TPU v7x, 1024 devices: a whole 4x4x32 slice. The times are simulated.
1024 devices in a mesh: seq: 64 (over z_lo, y, core), chan: 16 (over z_hi, x).
Axes of the slice: x: 4, y: 4, z: 32 (z_hi: 4, z_lo: 8; z = z_hi * 8 + z_lo), core: 2. Of those that a mesh axis runs over, the one named last changes fastest.
Arguments:
- out_grads: bfloat16 [8192, 4096], P(('seq', 'chan')), may hold values from -6 to 6
- layer_inputs: bfloat16 [8192, 4096], P('seq', 'chan'), may hold values from -0.015625 to 0.015625
- filters: bfloat16 [512, 256], P('seq', 'chan'), may hold values from -0.25 to 0.25
Outputs:
- input_grads: bfloat16 [8192, 4096], P('seq', 'chan')
- filter_grads: float32 [512, 256], P('seq', 'chan')
All inputs are finite; a program needn't handle non-finite values.
Results may differ from a plain program's by a relative error of at most 0.001.
Values may be sent and summed in bfloat16 or wider, within the bound.
A program may use at most 32 MiB of HBM per device.

v0:
```python
import jax
import jax.numpy as jnp
from jax import lax
from jax.sharding import PartitionSpec as P


def sent_to_all(x, axis):
    length = lax.axis_size(axis)
    return lax.all_to_all(jnp.broadcast_to(x[None], (length, *x.shape)), axis, 0, 0, tiled=True)


def joined_along(tiles, dim):
    shape = list(tiles.shape[1:])
    shape[dim] *= tiles.shape[0]
    return jnp.moveaxis(tiles, 0, dim).reshape(shape)


def collect(x, axis, dim):
    tiles = sent_to_all(x, axis)
    return joined_along(tiles, dim)


def shifted(value, axis, steps):
    count = lax.axis_size(axis)
    pairs = [(source, (source + steps) % count) for source in range(count)]
    return lax.ppermute(value, axis, pairs)


def in_blocks(x, dim, length):
    shape = x.shape
    tiles = x.reshape(*shape[:dim], length, shape[dim] // length, *shape[dim + 1 :])
    return jnp.moveaxis(tiles, dim, 0)


def summed_on_arrival(x, axis, dim):
    tiles = in_blocks(x, dim, lax.axis_size(axis))
    arrived = lax.all_to_all(tiles, axis, split_axis=0, concat_axis=0, tiled=True)
    return arrived.sum(axis=0)


def skewed_sums(products):
    groups_here, length, _ = products.shape
    padded = jnp.pad(products, ((0, 0), (0, 0), (0, length)))
    flat = padded.reshape(groups_here, 2 * length * length)[:, : length * (2 * length - 1)]
    return flat.reshape(groups_here, length, 2 * length - 1).sum(axis=1)


def on_device(out_grads, layer_inputs, filters):
    local_grads = lax.all_to_all(out_grads, "chan", split_axis=1, concat_axis=0, tiled=True)
    taps_all = collect(filters, "seq", 0)
    block_len = local_grads.shape[0]
    chan_width = local_grads.shape[1]
    groups_here = filters.shape[1]
    per_group = chan_width // groups_here
    taps_total = taps_all.shape[0]
    spread_blocks = taps_total // block_len
    filt_rows = taps_all.T
    x_reversed = layer_inputs[::-1].reshape(block_len, groups_here, per_group).transpose(1, 2, 0)
    offsets = lax.broadcasted_iota(jnp.int32, (block_len, block_len), 1) - lax.broadcasted_iota(
        jnp.int32, (block_len, block_len), 0
    )
    dx_total = jnp.zeros((groups_here, per_group, block_len), jnp.float32)
    lag_buffer = jnp.zeros((groups_here, (spread_blocks + 2) * block_len), jnp.float32)
    current = local_grads
    for lag_block in range(spread_blocks + 1):
        if lag_block > 0:
            current = shifted(local_grads, "seq", -lag_block)
        dy_grouped = current.reshape(block_len, groups_here, per_group).transpose(1, 2, 0)
        lag_index = lag_block * block_len + offsets
        inside = (lag_index >= 0) & (lag_index < taps_total)
        picked = jnp.take(filt_rows, jnp.clip(lag_index, 0, taps_total - 1), axis=1)
        toeplitz = jnp.where(inside[None], picked, jnp.zeros((), jnp.bfloat16))
        dx_total = dx_total + jnp.einsum(
            "guv,gkv->gku", toeplitz, dy_grouped, preferred_element_type=jnp.float32
        )
        products = jnp.einsum(
            "gku,gkv->guv", x_reversed, dy_grouped, preferred_element_type=jnp.float32
        )
        start = lag_block * block_len
        lag_buffer = lag_buffer.at[:, start : start + 2 * block_len - 1].add(skewed_sums(products))
    partial_dh = lag_buffer[:, block_len - 1 : block_len - 1 + taps_total].T
    filter_grads = summed_on_arrival(partial_dh, "seq", 0)
    input_grads = dx_total.transpose(2, 0, 1).reshape(block_len, chan_width).astype(jnp.bfloat16)
    return (input_grads, filter_grads)


def solution(mesh):
    in_specs = (P(("seq", "chan"), None), P("seq", "chan"), P("seq", "chan"))
    out_specs = (P("seq", "chan"), P("seq", "chan"))
    return jax.shard_map(
        on_device, mesh=mesh, in_specs=in_specs, out_specs=out_specs, check_vma=False
    )
```

profile of v0, /device:TPU:1, one launch (start us, length us, event | category | flops | bytes accessed | tf_op | source)
XLA Modules:
  0.0 458.9 jit_solution(6631057431459003713)
XLA Ops:
  2.0 18.2 %all-to-all-start = ((bf16[64,8,16]{2,1,0:T(8,128)(2,1)}), bf16[64,8,16]{2,1,0:T(8,128)(2,1)S(1)}, u32[]{:S(2)}, u32[]{:S(2)}) async-start(bf16[64,8,16]{2,1,0:T(8,128)(2,1)} %broadcast_in_dim.58), calls=%async_computation | async-start | bytes 262144 | tf_op jit(solution)/shard_map/all_to_all | solution.py:9
  22.2 12.7 %all-to-all-done = bf16[64,8,16]{2,1,0:T(8,128)(2,1)S(1)} async-done(((bf16[64,8,16]{2,1,0:T(8,128)(2,1)}), bf16[64,8,16]{2,1,0:T(8,128)(2,1)S(1)}, u32[]{:S(2)}, u32[]{:S(2)}) %all-to-all-start) | async-done | bytes 16416 | tf_op jit(solution)/shard_map/all_to_all | solution.py:9
  34.9 22.0 %all-to-all-start.1 = ((bf16[8,16,256]{2,0,1:T(8,128)(2,1)}), bf16[8,16,256]{2,0,1:T(8,128)(2,1)S(1)}, u32[]{:S(2)}, u32[]{:S(2)}) async-start(bf16[8,16,256]{2,0,1:T(8,128)(2,1)} %bitcast.125), calls=%async_computation.1 | async-start | bytes 131072 | tf_op jit(solution)/shard_map/all_to_all | solution.py:49
  62.0 57.4 %gather_fusion = bf16[16384,16]{1,0:T(8,128)(2,1)} fusion(bf16[16,512]{0,1:T(8,128)(2,1)S(1)} %bitcast.86, s32[16384]{0:T(1024)S(1)} %bitcast_clamp_fusion.4), kind=kCustom, calls=%fused_computation.clone | custom fusion | bytes 1114112 | tf_op jit(solution)/shard_map/jit(_take)/gather | solution.py:71
  119.4 3.7 copy.25
  123.1 57.4 %gather_fusion.1 = bf16[16384,16]{1,0:T(8,128)(2,1)} fusion(bf16[16,512]{0,1:T(8,128)(2,1)S(1)} %bitcast.87, s32[16384]{0:T(1024)S(1)} %bitcast_clamp_fusion.3), kind=kCustom, calls=%fused_computation.1.clone | custom fusion | bytes 1114112 | tf_op jit(solution)/shard_map/jit(_take)/gather | solution.py:71
  180.5 4.7 %copy.27 = bf16[128,128,16]{1,0,2:T(8,128)(2,1)} copy(bf16[128,128,16]{2,1,0:T(8,128)(2,1)} %bitcast.103) | data formatting | bytes 1048576 | tf_op jit(solution)/shard_map/jit(_take)/gather | solution.py:71
  185.2 57.4 %gather_fusion.3 = bf16[16384,16]{1,0:T(8,128)(2,1)} fusion(bf16[16,512]{0,1:T(8,128)(2,1)S(1)} %bitcast.88, s32[16384]{0:T(1024)S(1)} %bitcast_clamp_fusion.1), kind=kCustom, calls=%fused_computation.3.clone | custom fusion | bytes 1114112 | tf_op jit(solution)/shard_map/jit(_take)/gather | solution.py:71
  242.6 4.6 %copy.31 = bf16[128,128,16]{1,0,2:T(8,128)(2,1)} copy(bf16[128,128,16]{2,1,0:T(8,128)(2,1)} %bitcast.104) | data formatting | bytes 1048576 | tf_op jit(solution)/shard_map/jit(_take)/gather | solution.py:71
  247.2 57.4 %gather_fusion.4 = bf16[16384,16]{1,0:T(8,128)(2,1)} fusion(bf16[16,512]{0,1:T(8,128)(2,1)S(1)} %bitcast.89, s32[16384]{0:T(1024)S(1)} %bitcast_clamp_fusion), kind=kCustom, calls=%fused_computation.4.clone | custom fusion | bytes 1114112 | tf_op jit(solution)/shard_map/jit(_take)/gather | solution.py:71
  304.6 4.6 %copy.33 = bf16[128,128,16]{1,0,2:T(8,128)(2,1)} copy(bf16[128,128,16]{2,1,0:T(8,128)(2,1)} %bitcast.105) | data formatting | bytes 1048576 | tf_op jit(solution)/shard_map/jit(_take)/gather | solution.py:71
  309.2 57.4 %gather_fusion.2 = bf16[16384,16]{1,0:T(8,128)(2,1)} fusion(bf16[16,512]{0,1:T(8,128)(2,1)S(1)} %bitcast.90, s32[16384]{0:T(1024)S(1)} %bitcast_clamp_fusion.2), kind=kCustom, calls=%fused_computation.2.clone | custom fusion | bytes 1114112 | tf_op jit(solution)/shard_map/jit(_take)/gather | solution.py:71
  366.6 4.6 %copy.29 = bf16[128,128,16]{1,0,2:T(8,128)(2,1)} copy(bf16[128,128,16]{2,1,0:T(8,128)(2,1)} %bitcast.101) | data formatting | bytes 1048576 | tf_op jit(solution)/shard_map/jit(_take)/gather | solution.py:71
  371.2 2.6 collective-permute-start
  373.8 4.9 %collective-permute-start.1 = (bf16[128,256]{1,0:T(8,128)(2,1)S(1)}, bf16[128,256]{1,0:T(8,128)(2,1)S(1)}, u32[]{:S(2)}, u32[]{:S(2)}) collective-permute-start(bf16[128,256]{1,0:T(8,128)(2,1)S(1)} %bitcast.113), channel_id=1, source_target_pairs={{0,992},{16,1008},{32,0},{48,16},{64,32},{80,48},{96,64},{112,80},... | collective-permute-start | bytes 196616 | tf_op jit(solution)/shard_map/ppermute | solution.py:26
  378.7 3.3 collective-permute-start.2
  381.9 4.0 collective-permute-start.3
  390.1 4.8 %reshape.238 = f32[16,128,255]{2,1,0:T(8,128)S(1)} reshape(f32[16,32640]{1,0:T(8,128)} %slice.130) | data formatting | bytes 4177920 | tf_op jit(solution)/shard_map/reshape | solution.py:45
  402.1 4.8 %reshape.240 = f32[16,128,255]{2,1,0:T(8,128)S(1)} reshape(f32[16,32640]{1,0:T(8,128)} %slice.131) | data formatting | bytes 4177920 | tf_op jit(solution)/shard_map/reshape | solution.py:45
  411.3 5.0 %reshape.242 = f32[16,128,255]{2,1,0:T(8,128)S(1)} reshape(f32[16,32640]{1,0:T(8,128)} %slice.133) | data formatting | bytes 4177920 | tf_op jit(solution)/shard_map/reshape | solution.py:45
  420.0 4.8 %reshape.244 = f32[16,128,255]{2,1,0:T(8,128)S(1)} reshape(f32[16,32640]{1,0:T(8,128)} %slice.135) | data formatting | bytes 4177920 | tf_op jit(solution)/shard_map/reshape | solution.py:45
  429.9 4.8 %reshape.246 = f32[16,128,255]{2,1,0:T(8,128)S(1)} reshape(f32[16,32640]{1,0:T(8,128)} %slice.137) | data formatting | bytes 4177920 | tf_op jit(solution)/shard_map/reshape | solution.py:45
  439.9 4.5 all-to-all-start.2
  447.6 9.2 %all-to-all-done.2 = f32[64,1,128]{2,1,0:T(1,128)S(1)} async-done(((f32[64,1,128]{2,1,0:T(1,128)}), f32[64,1,128]{2,1,0:T(1,128)S(1)}, u32[]{:S(2)}, u32[]{:S(2)}) %all-to-all-start.2) | async-done | bytes 32800 | tf_op jit(solution)/shard_map/all_to_all | solution.py:37
  (103 shorter events, 42.9 us)
Async XLA Ops:
  2.0 33.0 %all-to-all-start = ((bf16[64,8,16]{2,1,0:T(8,128)(2,1)}), bf16[64,8,16]{2,1,0:T(8,128)(2,1)S(1)}, u32[]{:S(2)}, u32[]{:S(2)}) async-start(bf16[64,8,16]{2,1,0:T(8,128)(2,1)} %broadcast_in_dim.58), calls=%async_computation | async-start | bytes 262144 | tf_op jit(solution)/shard_map/all_to_all | solution.py:9
  34.9 336.3 %all-to-all-start.1 = ((bf16[8,16,256]{2,0,1:T(8,128)(2,1)}), bf16[8,16,256]{2,0,1:T(8,128)(2,1)S(1)}, u32[]{:S(2)}, u32[]{:S(2)}) async-start(bf16[8,16,256]{2,0,1:T(8,128)(2,1)} %bitcast.125), calls=%async_computation.1 | async-start | bytes 131072 | tf_op jit(solution)/shard_map/all_to_all | solution.py:49
  371.2 25.6 %collective-permute-start = (bf16[128,256]{1,0:T(8,128)(2,1)S(1)}, bf16[128,256]{1,0:T(8,128)(2,1)S(1)}, u32[]{:S(2)}, u32[]{:S(2)}) collective-permute-start(bf16[128,256]{1,0:T(8,128)(2,1)S(1)} %bitcast.112), channel_id=1, source_target_pairs={{0,1008},{16,0},{32,16},{48,32},{64,48},{80,64},{96,80},{112,96},{... | collective-permute-start | bytes 196616 | tf_op jit(solution)/shard_map/ppermute | solution.py:26
  373.8 23.5 %collective-permute-start.1 = (bf16[128,256]{1,0:T(8,128)(2,1)S(1)}, bf16[128,256]{1,0:T(8,128)(2,1)S(1)}, u32[]{:S(2)}, u32[]{:S(2)}) collective-permute-start(bf16[128,256]{1,0:T(8,128)(2,1)S(1)} %bitcast.113), channel_id=1, source_target_pairs={{0,992},{16,1008},{32,0},{48,16},{64,32},{80,48},{96,64},{112,80},... | collective-permute-start | bytes 196616 | tf_op jit(solution)/shard_map/ppermute | solution.py:26
  378.7 20.1 %collective-permute-start.2 = (bf16[128,256]{1,0:T(8,128)(2,1)S(1)}, bf16[128,256]{1,0:T(8,128)(2,1)S(1)}, u32[]{:S(2)}, u32[]{:S(2)}) collective-permute-start(bf16[128,256]{1,0:T(8,128)(2,1)S(1)} %bitcast.114), channel_id=1, source_target_pairs={{0,976},{16,992},{32,1008},{48,0},{64,16},{80,32},{96,48},{112,64}... | collective-permute-start | bytes 196616 | tf_op jit(solution)/shard_map/ppermute | solution.py:26
  381.9 43.7 %collective-permute-start.3 = (bf16[128,256]{1,0:T(8,128)(2,1)S(1)}, bf16[128,256]{1,0:T(8,128)(2,1)}, u32[]{:S(2)}, u32[]{:S(2)}) collective-permute-start(bf16[128,256]{1,0:T(8,128)(2,1)S(1)} %bitcast.115), channel_id=1, source_target_pairs={{0,960},{16,976},{32,992},{48,1008},{64,0},{80,16},{96,32},{112,48... | collective-permute-start | bytes 196616 | tf_op jit(solution)/shard_map/ppermute | solution.py:26
  434.7 1.4 copy-start.4
  434.7 2.5 copy-start.5
  434.7 9.7 %copy-start.3 = (bf16[128,128,16]{1,0,2:T(8,128)(2,1)S(1)}, bf16[128,128,16]{1,0,2:T(8,128)(2,1)}, u32[]{:S(2)}) copy-start(bf16[128,128,16]{1,0,2:T(8,128)(2,1)} %copy.31) | copy-start | bytes 1572868
  434.7 10.9 %copy-start = (bf16[128,128,16]{1,0,2:T(8,128)(2,1)S(1)}, bf16[128,128,16]{1,0,2:T(8,128)(2,1)}, u32[]{:S(2)}) copy-start(bf16[128,128,16]{1,0,2:T(8,128)(2,1)} %copy.27) | copy-start | bytes 1572868
  434.9 10.7 %copy-start.6 = (pred[128,128]{1,0:T(8,128)(4,1)S(1)}, pred[128,128]{1,0:T(8,128)(4,1)}, u32[]{:S(2)}) copy-start(pred[128,128]{1,0:T(8,128)(4,1)} %get-tuple-element.75) | copy-start | bytes 49156
  434.9 10.8 %copy-start.7 = (pred[128,128]{1,0:T(8,128)(4,1)S(1)}, pred[128,128]{1,0:T(8,128)(4,1)}, u32[]{:S(2)}) copy-start(pred[128,128]{1,0:T(8,128)(4,1)} %get-tuple-element.76) | copy-start | bytes 49156
  434.9 10.8 %copy-start.12 = (f32[16,128,16]{1,2,0:T(8,128)S(1)}, f32[16,128,16]{1,2,0:T(8,128)}, u32[]{:S(2)}) copy-start(f32[16,128,16]{1,2,0:T(8,128)} %fusion.5) | copy-start | bytes 393220
  436.1 10.0 %copy-start.2 = (bf16[128,128,16]{1,0,2:T(8,128)(2,1)S(1)}, bf16[128,128,16]{1,0,2:T(8,128)(2,1)}, u32[]{:S(2)}) copy-start(bf16[128,128,16]{1,0,2:T(8,128)(2,1)} %copy.33) | copy-start | bytes 1572868
  436.1 10.0 %copy-start.8 = (pred[128,128]{1,0:T(8,128)(4,1)S(1)}, pred[128,128]{1,0:T(8,128)(4,1)}, u32[]{:S(2)}) copy-start(pred[128,128]{1,0:T(8,128)(4,1)} %get-tuple-element.69) | copy-start | bytes 49156
  436.1 10.0 %copy-start.9 = (pred[128,128]{1,0:T(8,128)(4,1)S(1)}, pred[128,128]{1,0:T(8,128)(4,1)}, u32[]{:S(2)}) copy-start(pred[128,128]{1,0:T(8,128)(4,1)} %get-tuple-element.70) | copy-start | bytes 49156
  439.9 16.9 %all-to-all-start.2 = ((f32[64,1,128]{2,1,0:T(1,128)}), f32[64,1,128]{2,1,0:T(1,128)S(1)}, u32[]{:S(2)}, u32[]{:S(2)}) async-start(f32[64,1,128]{2,1,0:T(1,128)} %reshape.318), calls=%async_computation.2 | async-start | bytes 65536 | tf_op jit(solution)/shard_map/all_to_all | solution.py:37
  444.4 2.0 copy-start.1
  444.5 2.0 copy-start.10
  444.5 2.0 copy-start.11
where the time goes:
time: 460 us; the launch traced here: 459 us
  local copies, waits for them, and re-layouts  358 us (78%)
  starting transfers between devices  59.4 us (13%)
  waiting for transfers between devices  21.9 us (5%)
  other arithmetic  12.6 us (3%)
  matrix products  6.04 us (1%)
    gather x10, local copies, waits for them, and re-layouts, on_device(): picked = jnp.take(filt_rows, jnp.clip(lag_index, 0, taps_total - 1), axis=1)  309 us
    reshape x5, local copies, waits for them, and re-layouts, skewed_sums(): return flat.reshape(groups_here, length, 2 * length - 1).sum(axis=1)  24.3 us
    all_to_all x1, starting transfers between devices, on_device(): lax.all_to_all(out_grads, 'chan', split_axis=1, concat_axis=0, tiled=True)  22 us
    all_to_all x1, starting transfers between devices, sent_to_all(): lax.all_to_all(jnp.broadcast_to(x[None], (length, *x.shape)), axis, 0, 0,...  18.2 us
    ppermute x4, starting transfers between devices, shifted(): return lax.ppermute(value, axis, pairs)  14.7 us
    all_to_all x1, waiting for transfers between devices, sent_to_all(): lax.all_to_all(jnp.broadcast_to(x[None], (length, *x.shape)), axis, 0, 0,...  12.7 us
    all_to_all x1, waiting for transfers between devices, summed_on_arrival(): lax.all_to_all(tiles, axis, split_axis=0, concat_axis=0, tiled=True)  9.21 us
  transfers between devices with their start and end apart: 7, of which 2 were waited for; matrix products, arithmetic and copies ran while one was open for 78% of the time, Pallas kernels for 0%

commit v1 on v0

v1 whole, which is shorter than its diff:
```python
import functools

import jax
import jax.numpy as jnp
from jax import lax
from jax.experimental import pallas as pl
from jax.experimental.pallas import tpu as pltpu
from jax.sharding import PartitionSpec as P

MESH = pl.DeviceIdType.MESH
LANES = 128
INNER = 8
CROSS = 4
GANG = 4


def kernel(ns, nc, dy_hbm, x_hbm, filt_ref, dx_hbm, dh_ref,
           dy_buf, dyc, x_buf, x_rev, row_buf, tile_buf, gathered, unpacked, frow, toep, dh_rows, dh_cols,
           packed, rs1, mid, rs2, dx_buf,
           s_a2a, r_a2a, s_row, r_row, s_tile, r_tile, s_halo, r_halo, s_rs1, r_rs1, s_rs2, r_rs2, s_loc):
    f32, bf16 = jnp.float32, jnp.bfloat16
    outer, zs = ns // INNER, nc // CROSS
    rows, width = dy_buf.shape[2], dy_buf.shape[3]
    block = rows * nc
    reach = dy_buf.shape[0] - 1
    span = (reach + 1) * block
    taps = reach * block
    groups = filt_ref.shape[1]
    per = width // groups
    s, c = lax.axis_index("seq"), lax.axis_index("chan")
    zo, yc = s // INNER, lax.rem(s, INNER)
    zh, xx = c // CROSS, lax.rem(c, CROSS)

    def chan_peer(dz, dx):
        return lax.rem(zh + dz, zs) * CROSS + lax.rem(xx + dx, CROSS)

    def inner_peer(j):
        return zo * INNER + lax.rem(yc + j, INNER)

    def outer_peer(j):
        return lax.rem(zo + j, outer) * INNER + yc

    def send(src, dst, ssem, rsem, seq, chan):
        copy = pltpu.make_async_remote_copy(
            src_ref=src, dst_ref=dst, send_sem=ssem, recv_sem=rsem, device_id=(seq, chan), device_id_type=MESH)
        copy.start()
        return copy

    hops = [(dz, dx) for dz in sorted(range(zs), key=lambda d: -min(d, zs - d)) for dx in range(CROSS) if dz or dx]
    order = sorted(range(zs), key=lambda d: min(d, zs - d))

    barrier = pltpu.get_barrier_semaphore()
    friends = [(s, chan_peer(dz, dx)) for dz, dx in hops]
    friends += [(inner_peer(j), c) for j in range(1, INNER)]
    friends += [(outer_peer(j), c) for j in range(1, outer)]
    for k in range(1, reach + 1):
        friends += [(lax.rem(s + k, ns), c), (lax.rem(s + ns - k, ns), c)]
    for friend in friends:
        pl.semaphore_signal(barrier, inc=1, device_id=friend, device_id_type=MESH)

    own = pltpu.make_async_copy(
        dy_hbm.at[:, pl.ds(pl.multiple_of(c * width, width), width)], dy_buf.at[0, c], s_loc.at[0])
    own.start()
    x_in = pltpu.make_async_copy(x_hbm, x_buf, s_loc.at[1])
    x_in.start()

    unpacked[...] = jnp.zeros_like(unpacked)
    unpacked[0:8, 0:groups] = filt_ref[...].astype(f32)
    flat = jnp.sum(pltpu.roll(unpacked[0:8, :], 0, 1, stride=groups, stride_axis=0), axis=0, keepdims=True)
    row_buf[yc] = flat

    pl.semaphore_wait(barrier, len(friends))

    sent = []
    for dz, dx in hops:
        peer = chan_peer(dz, dx)
        sent.append(send(dy_hbm.at[:, pl.ds(pl.multiple_of(peer * width, width), width)], dy_buf.at[0, c],
                         s_a2a.at[dz, dx], r_a2a.at[dz, dx], s, peer))
    row_sends = [send(row_buf.at[yc], row_buf.at[yc], s_row.at[j], r_row.at[j], inner_peer(j), c)
                 for j in range(1, INNER)]
    for copy in row_sends:
        copy.wait()
    for i in range(INNER):
        tile_buf[zo, i:i + 1, :] = row_buf[i]
    tile_sends = [send(tile_buf.at[zo], tile_buf.at[zo], s_tile.at[j], r_tile.at[j], outer_peer(j), c)
                  for j in range(1, outer)]

    own.wait()
    a2a = dict(zip(hops, sent))
    halo = []
    for dz in order:
        for dx in range(CROSS):
            if dz or dx:
                a2a[dz, dx].wait()
        first = lax.rem(zh + zs - dz, zs) * CROSS
        for k in range(1, reach + 1):
            halo.append(send(dy_buf.at[0, pl.ds(first, CROSS)], dy_buf.at[k, pl.ds(first, CROSS)],
                             s_halo.at[k - 1, dz], r_halo.at[k - 1, dz], lax.rem(s + ns - k, ns), c))

    x_in.wait()
    r0 = lax.broadcasted_iota(jnp.int32, (block, block), 0)
    r1 = lax.broadcasted_iota(jnp.int32, (block, block), 1)
    flip = jnp.where(r0 + r1 == block - 1, 1.0, 0.0).astype(bf16)
    x_rev[...] = jnp.dot(flip, x_buf[...], preferred_element_type=f32).astype(bf16)

    for copy in tile_sends:
        copy.wait()
    gathered[...] = tile_buf[...].reshape(outer * INNER, LANES)
    for t in range(8):
        turned = gathered[...] if t == 0 else pltpu.roll(gathered[...], LANES - t * groups, 1)
        unpacked[pl.ds(t, taps // 8, stride=8), :] = turned
    frow[...] = jnp.zeros_like(frow)
    for b in range(taps // LANES):
        frow[:, b * LANES:(b + 1) * LANES] = unpacked[b * LANES:(b + 1) * LANES, :].T[0:groups, :]

    def build(g, _):
        wide = jnp.broadcast_to(frow[pl.ds(g, 1), :], (block, span))
        toep[g] = pltpu.roll(wide, 0, 1, stride=1, stride_axis=0).astype(bf16)
        return 0

    lax.fori_loop(0, groups, build, 0)

    for copy in halo:
        copy.wait()
    for k in range(reach + 1):
        dyc[k * block:(k + 1) * block, :] = dy_buf[k].astype(f32).reshape(block, width).astype(bf16)

    lane_group = lax.broadcasted_iota(jnp.int32, (block, width), 1) // per
    dh_rows[...] = jnp.zeros_like(dh_rows)

    def correlate(i, _):
        xr = x_rev[...]
        masked = jnp.concatenate(
            [jnp.where(lane_group == i * GANG + q, xr, jnp.zeros_like(xr)) for q in range(GANG)], axis=0)
        products = lax.dot_general(masked, dyc[...], (((1,), (1,)), ((), ())), preferred_element_type=f32)
        for q in range(GANG):
            skewed = pltpu.roll(products[q * block:(q + 1) * block, :], 0, 1, stride=1, stride_axis=0)
            dh_rows[pl.ds(i * GANG + q, 1), :] = jnp.sum(skewed, axis=0, keepdims=True)
        return 0

    lax.fori_loop(0, groups // GANG, correlate, 0)
    aligned = pltpu.roll(dh_rows[...], span - (block - 1), 1)
    for b in range(taps // LANES):
        dh_cols[b * LANES:(b + 1) * LANES, :] = aligned[:, b * LANES:(b + 1) * LANES].T
    rows_packed = dh_cols[pl.ds(0, taps // 8, stride=8), :]
    for t in range(1, 8):
        rows_packed = rows_packed + pltpu.roll(dh_cols[pl.ds(t, taps // 8, stride=8), :], t * groups, 1)
    packed[...] = rows_packed.reshape(outer, INNER, LANES)
    rs1[0] = packed[zo]
    rs1_sends = []
    for j in range(1, outer):
        peer = lax.rem(zo + j, outer)
        rs1_sends.append(send(packed.at[peer], rs1.at[j], s_rs1.at[j], r_rs1.at[j], peer * INNER + yc, c))

    def convolve(i, acc):
        filters = toep[pl.ds(i * GANG, GANG)].reshape(GANG * block, span)
        out = jnp.dot(filters, dyc[...], preferred_element_type=f32)
        for q in range(GANG):
            acc = jnp.where(lane_group == i * GANG + q, out[q * block:(q + 1) * block, :], acc)
        return acc

    dx_buf[...] = lax.fori_loop(0, groups // GANG, convolve, jnp.zeros((block, width), f32)).astype(bf16)
    dx_out = pltpu.make_async_copy(dx_buf, dx_hbm, s_loc.at[2])
    dx_out.start()

    for copy in rs1_sends:
        copy.wait()
    mid[...] = jnp.sum(rs1[...], axis=0)
    rs2_sends = [send(mid, rs2.at[j], s_rs2.at[j], r_rs2.at[j], inner_peer(j), c) for j in range(1, INNER)]
    rs2[0] = mid[...]
    for copy in rs2_sends:
        copy.wait()
    mine = rs2[0, pl.ds(yc, 1), :]
    for j in range(1, INNER):
        mine = mine + rs2[j, pl.ds(yc, 1), :]
    for t in range(8):
        dh_ref[t:t + 1, :] = mine[:, t * groups:(t + 1) * groups]
    dx_out.wait()


def on_device(ns, nc, dy, x, filt):
    rows, width = dy.shape[0], x.shape[1]
    block = x.shape[0]
    groups = filt.shape[1]
    taps = filt.shape[0] * ns
    reach = taps // block
    span = taps + block
    outer, zs = ns // INNER, nc // CROSS
    f32, bf16 = jnp.float32, jnp.bfloat16
    vmem, dma = pltpu.VMEM, pltpu.SemaphoreType.DMA
    return pl.pallas_call(
        functools.partial(kernel, ns, nc),
        out_shape=(jax.ShapeDtypeStruct(x.shape, bf16), jax.ShapeDtypeStruct(filt.shape, f32)),
        in_specs=[pl.BlockSpec(memory_space=pl.ANY), pl.BlockSpec(memory_space=pl.ANY),
                  pl.BlockSpec(memory_space=pltpu.VMEM)],
        out_specs=(pl.BlockSpec(memory_space=pl.ANY), pl.BlockSpec(memory_space=pltpu.VMEM)),
        scratch_shapes=[
            vmem((reach + 1, nc, rows, width), bf16),
            vmem((span, width), bf16),
            vmem((block, width), bf16),
            vmem((block, width), bf16),
            vmem((INNER, 1, LANES), f32),
            vmem((outer, INNER, LANES), f32),
            vmem((ns, LANES), f32),
            vmem((taps, LANES), f32),
            vmem((groups, span), f32),
            vmem((groups, block, span), bf16),
            vmem((LANES, span), f32),
            vmem((taps, LANES), f32),
            vmem((outer, INNER, LANES), f32),
            vmem((outer, INNER, LANES), f32),
            vmem((INNER, LANES), f32),
            vmem((INNER, INNER, LANES), f32),
            vmem((block, width), bf16),
            dma((zs, CROSS)), dma((zs, CROSS)),
            dma((INNER,)), dma((INNER,)),
            dma((outer,)), dma((outer,)),
            dma((reach, zs)), dma((reach, zs)),
            dma((outer,)), dma((outer,)),
            dma((INNER,)), dma((INNER,)),
            dma((3,)),
        ],
        compiler_params=pltpu.CompilerParams(
            collective_id=0, has_side_effects=True, vmem_limit_bytes=40 * 2**20),
    )(dy, x, filt)


def solution(mesh):
    ns, nc = mesh.shape["seq"], mesh.shape["chan"]
    in_specs = (P(("seq", "chan"), None), P("seq", "chan"), P("seq", "chan"))
    out_specs = (P("seq", "chan"), P("seq", "chan"))
    return jax.shard_map(
        functools.partial(on_device, ns, nc), mesh=mesh, in_specs=in_specs, out_specs=out_specs, check_vma=False)
```

time: 460 us -> 66.3 us (0.14)
  local copies, waits for them, and re-layouts: 358 us -> 3.58 us
  Pallas kernels: 0 us -> 61.8 us
  starting transfers between devices: 59.4 us -> 0 us
  waiting for transfers between devices: 21.9 us -> 0 us
  other arithmetic: 12.6 us -> 0 us
  matrix products: 6.04 us -> 0 us
    gather x10 -> x0, local copies, waits for them, and re-layouts: 309 us -> none  [on_device(): picked = jnp.take(filt_rows, jnp.clip(lag_index, 0, taps_total - 1), axis=1)]
    pallas_call x0 -> x1, Pallas kernels: none -> 61.8 us  [on_device(): pl.pallas_call(functools.partial(kernel, ns, nc), out_shape=(jax.ShapeDty...]
    all_to_all x3 -> x0, starting transfers between devices: 44.7 us -> none  [the longest x1 22 us: on_device(): lax.all_to_all(out_grads, 'chan', split_axis=1, concat_axis=0, tiled=True)]
    reshape x7 -> x0, local copies, waits for them, and re-layouts: 25.1 us -> none  [the longest x5 24.3 us: skewed_sums(): return flat.reshape(groups_here, length, 2 * length - 1).sum(axis=1)]
    all_to_all x3 -> x0, waiting for transfers between devices: 21.9 us -> none  [the longest x1 12.7 us: sent_to_all(): lax.all_to_all(jnp.broadcast_to(x[None], (length, *x.shape)), axis, 0, 0,...]
    ppermute x4 -> x0, starting transfers between devices: 14.7 us -> none  [shifted(): return lax.ppermute(value, axis, pairs)]
    slice x5 -> x0, local copies, waits for them, and re-layouts: 7.43 us -> none  [skewed_sums(): padded.reshape(groups_here, 2 * length * length)]
    another operation x10 -> x0, other arithmetic: 6.52 us -> none
  transfers between devices with their start and end apart: 7 -> 0, of which waited for: 2 -> 0; matrix products, arithmetic and copies ran while one was open for 78% -> 0% of each run, Pallas kernels for 0% -> 0%
where the time goes in v1:
time: 66.3 us; the launch traced here: 66 us
  Pallas kernels  61.8 us (93%)
  local copies, waits for them, and re-layouts  3.58 us (5%)
    pallas_call x1, Pallas kernels, on_device(): pl.pallas_call(functools.partial(kernel, ns, nc), out_shape=(jax.ShapeDty...  61.8 us
    unnamed x8, local copies, waits for them, and re-layouts  3.58 us

profile of v1, /device:TPU:1, one launch (start us, length us, event | category | flops | bytes accessed | tf_op | source)
XLA Modules:
  0.0 66.0 jit_solution(15853840419019060822)
XLA Ops:
  0.6 0.0 copy-start
  0.6 0.8 %copy-done = bf16[8,4096]{1,0:T(8,128)(2,1)S(1)} copy-done((bf16[8,4096]{1,0:T(8,128)(2,1)S(1)}, bf16[8,4096]{1,0:T(8,128)(2,1)}, u32[]{:S(2)}) %copy-start) | copy-done | bytes 65560
  1.5 0.0 copy-start.1
  1.5 0.8 %copy-done.1 = bf16[128,256]{1,0:T(8,128)(2,1)S(1)} copy-done((bf16[128,256]{1,0:T(8,128)(2,1)S(1)}, bf16[128,256]{1,0:T(8,128)(2,1)}, u32[]{:S(2)}) %copy-start.1) | copy-done | bytes 65560
  2.3 0.0 copy-start.2
  2.3 0.7 %copy-done.2 = bf16[8,16]{1,0:T(8,128)(2,1)S(1)} copy-done((bf16[8,16]{1,0:T(8,128)(2,1)S(1)}, bf16[8,16]{1,0:T(8,128)(2,1)}, u32[]{:S(2)}) %copy-start.2) | copy-done | bytes 280
  3.0 61.8 %shard_map.50 = (bf16[128,256]{1,0:T(8,128)(2,1)S(1)}, f32[8,16]{1,0:T(8,128)S(1)}) custom-call(bf16[8,4096]{1,0:T(8,128)(2,1)S(1)} %copy-done, bf16[128,256]{1,0:T(8,128)(2,1)S(1)} %copy-done.1, bf16[8,16]{1,0:T(8,128)(2,1)S(1)} %copy-done.2), custom_call_target="tpu_custom_call" | custom-call | tf_op jit(solution)/shard_map/pallas_call | solution.py:191
  64.8 0.6 copy.7
  65.4 0.6 copy.8
Async XLA Ops:
  0.6 0.8 %copy-start = (bf16[8,4096]{1,0:T(8,128)(2,1)S(1)}, bf16[8,4096]{1,0:T(8,128)(2,1)}, u32[]{:S(2)}) copy-start(bf16[8,4096]{1,0:T(8,128)(2,1)} %dy_hbm.1) | copy-start | bytes 196612
  1.5 0.8 %copy-start.1 = (bf16[128,256]{1,0:T(8,128)(2,1)S(1)}, bf16[128,256]{1,0:T(8,128)(2,1)}, u32[]{:S(2)}) copy-start(bf16[128,256]{1,0:T(8,128)(2,1)} %x_hbm.1) | copy-start | bytes 196612
  2.3 0.7 %copy-start.2 = (bf16[8,16]{1,0:T(8,128)(2,1)S(1)}, bf16[8,16]{1,0:T(8,128)(2,1)}, u32[]{:S(2)}) copy-start(bf16[8,16]{1,0:T(8,128)(2,1)} %filt_ref.1) | copy-start | bytes 772

commit v2 on v1

v2 whole, which is shorter than its diff:
```python
import functools

import jax
import jax.numpy as jnp
from jax import lax
from jax.experimental import pallas as pl
from jax.experimental.pallas import tpu as pltpu
from jax.sharding import PartitionSpec as P

MESH = pl.DeviceIdType.MESH
LANES = 128
CROSS = 4
GANG = 4


def kernel(ns, nc, dy_hbm, x_hbm, filt_ref, dx_hbm, dh_ref,
           dy_buf, dyc, x_buf, x_half, x_ext, xw, row_buf, gathered, unpacked, frow, toep, dh_rows, dh_cols,
           staged, packed, rs, dx_out, dx_buf,
           s_a2a, r_a2a, s_x, r_x, s_row, r_row, s_halo, r_halo, s_rs, r_rs, s_dx, r_dx, s_loc):
    f32, bf16 = jnp.float32, jnp.bfloat16
    zs = nc // CROSS
    rows, half = dy_buf.shape[2], dy_buf.shape[3]
    block = rows * nc
    width = 2 * half
    quarter = block // zs
    span = dyc.shape[0]
    reach = span // block - 1
    taps = reach * block
    groups = filt_ref.shape[1]
    per = width // groups
    mine = groups // 2
    s, c = lax.axis_index("seq"), lax.axis_index("chan")
    e = lax.rem(s, 2)
    sib = s + 1 - 2 * e
    zh, xx = c // CROSS, lax.rem(c, CROSS)

    def chan_peer(dz, dx):
        return lax.rem(zh + dz, zs) * CROSS + lax.rem(xx + dx, CROSS)

    def copy_to(src, dst, ssem, rsem, seq, chan):
        return pltpu.make_async_remote_copy(
            src_ref=src, dst_ref=dst, send_sem=ssem, recv_sem=rsem, device_id=(seq, chan), device_id_type=MESH)

    def send(*args):
        copy = copy_to(*args)
        copy.start()
        return copy

    far = sorted(range(zs), key=lambda d: -min(d, zs - d))
    near = far[::-1]
    cores = ((0, s), (1, sib))

    barrier = pltpu.get_barrier_semaphore()
    friends = [(seq, chan_peer(dz, dx)) for dz in far for dx in range(CROSS) for _, seq in cores if dz or dx]
    for friend in friends:
        pl.semaphore_signal(barrier, inc=1, device_id=friend, device_id_type=MESH)

    def greet(j, _):
        pl.semaphore_signal(barrier, inc=1, device_id=(lax.rem(s + j, ns), c), device_id_type=MESH)
        return 0

    lax.fori_loop(1, ns, greet, 0)

    x_in = pltpu.make_async_copy(x_hbm, x_buf, s_loc.at[1])
    x_in.start()
    own = pltpu.make_async_copy(
        dy_hbm.at[:, pl.ds(pl.multiple_of(c * width + e * half, half), half)], dy_buf.at[e, c], s_loc.at[0])
    own.start()

    unpacked[...] = jnp.zeros_like(unpacked)
    unpacked[0:8, 0:groups] = filt_ref[...].astype(f32)
    row_buf[s] = jnp.sum(pltpu.roll(unpacked[0:8, :], 0, 1, stride=groups, stride_axis=0), axis=0, keepdims=True)
    frow[...] = jnp.zeros_like(frow)
    dh_rows[...] = jnp.zeros_like(dh_rows)

    x_in.wait()
    r0 = lax.broadcasted_iota(jnp.int32, (block, block), 0)
    r1 = lax.broadcasted_iota(jnp.int32, (block, block), 1)
    flip = jnp.where(r0 + r1 == block - 1, 1.0, 0.0).astype(bf16)
    for h in range(2):
        x_half[h] = jnp.dot(flip, x_buf[:, h * half:(h + 1) * half], preferred_element_type=f32).astype(bf16)
    x_ext[1 - e] = x_half[e]

    pl.semaphore_wait(barrier, len(friends) + ns - 1)

    a2a = {}
    for dz in far:
        for dx in range(CROSS):
            for r, seq in cores:
                if dz or dx or r:
                    peer = chan_peer(dz, dx)
                    their = e if r == 0 else 1 - e
                    start = pl.multiple_of(peer * width + their * half, half)
                    a2a[dz, dx, r] = send(dy_hbm.at[:, pl.ds(start, half)], dy_buf.at[e, c],
                                          s_a2a.at[dz, dx, r], r_a2a.at[dz, dx, r], seq, peer)
    x_sends = []
    for m in range(reach // 2 + 1):
        for r, seq in cores:
            if m or r:
                their = e if r == 0 else 1 - e
                x_sends.append(send(x_half.at[their], x_ext.at[2 * m + 1 - e],
                                    s_x.at[m, r], r_x.at[m, r], lax.rem(seq + 2 * m, ns), c))

    def send_row(j, _):
        copy_to(row_buf.at[s], row_buf.at[s], s_row, r_row, lax.rem(s + j, ns), c).start()
        return 0

    lax.fori_loop(1, ns, send_row, 0)
    all_rows = copy_to(row_buf.at[pl.ds(0, ns - 1)], row_buf.at[pl.ds(0, ns - 1)], s_row, r_row, sib, c)

    lane = lax.broadcasted_iota(jnp.int32, (quarter, width), 1)
    lane_group = lax.rem(lane, half) // per
    own.wait()
    halo = []
    total = jnp.zeros((mine, span), f32)
    for dz in near:
        for dx in range(CROSS):
            for r, _ in cores:
                if dz or dx or r:
                    a2a[dz, dx, r].wait_recv()
        zg = lax.rem(zh + zs - dz, zs)
        part = (pl.ds(0, 2), pl.ds(zg * CROSS, CROSS))
        for m in range(1, reach // 2 + 1):
            halo.append(send(dy_buf.at[part], dy_buf.at[pl.ds(2 * m, 2), pl.ds(zg * CROSS, CROSS)],
                             s_halo.at[m - 1, dz], r_halo.at[m - 1, dz], lax.rem(s + ns - 2 * m, ns), c))
        if dz == 0:
            for copy in x_sends:
                copy.wait_recv()
            for i in range(reach + 1):
                xw[i * block:(i + 1) * block, 0:half] = x_ext[i + 1]
                xw[i * block:(i + 1) * block, half:width] = x_ext[i]
        at = pl.ds(pl.multiple_of(zg * quarter, quarter), quarter)
        for b in range(2):
            chunk = dy_buf[b, pl.ds(zg * CROSS, CROSS)].astype(f32).reshape(quarter, half).astype(bf16)
            dyc[at, b * half:(b + 1) * half] = chunk
        grads = dyc[at, :]
        masked = jnp.concatenate(
            [jnp.where(lane_group == q, grads, jnp.zeros_like(grads)) for q in range(mine)], axis=0)
        products = lax.dot_general(masked, xw[...], (((1,), (1,)), ((), ())), preferred_element_type=f32)
        sums = []
        for q in range(mine):
            skewed = pltpu.roll(products[q * quarter:(q + 1) * quarter, :], 0, 1, stride=1, stride_axis=0)
            sums.append(jnp.sum(skewed, axis=0, keepdims=True))
        total = total + pltpu.roll(jnp.concatenate(sums, axis=0), zg * quarter, 1)

    dh_rows[pl.ds(pl.multiple_of(e * mine, mine), mine), :] = pltpu.roll(total, span - (block - 1), 1)
    for b in range(taps // LANES):
        dh_cols[b * LANES:(b + 1) * LANES, :] = dh_rows[:, b * LANES:(b + 1) * LANES].T
    rows_packed = dh_cols[pl.ds(0, ns, stride=8), :]
    for t in range(1, 8):
        rows_packed = rows_packed + pltpu.roll(dh_cols[pl.ds(t, ns, stride=8), :], t * groups, 1)
    staged[...] = rows_packed
    for i in range(ns):
        packed[i] = staged[i:i + 1, :]

    def send_terms(j, _):
        peer = lax.rem(s + j, ns)
        copy_to(packed.at[peer], rs.at[j], s_rs, r_rs, peer, c).start()
        return 0

    lax.fori_loop(1, ns, send_terms, 0)
    rs[0] = packed[s]
    all_terms = copy_to(packed.at[pl.ds(0, ns - 1)], rs.at[pl.ds(1, ns - 1)], s_rs, r_rs, sib, c)

    all_rows.wait_recv()
    for i in range(ns):
        gathered[i:i + 1, :] = row_buf[i]
    for t in range(8):
        turned = gathered[...] if t == 0 else pltpu.roll(gathered[...], LANES - t * groups, 1)
        unpacked[pl.ds(t, ns, stride=8), :] = turned
    for b in range(taps // LANES):
        frow[:, b * LANES:(b + 1) * LANES] = unpacked[b * LANES:(b + 1) * LANES, :].T[0:groups, :]

    def build(g, _):
        wide = jnp.broadcast_to(frow[pl.ds(e * mine + g, 1), :], (block, span))
        toep[g] = pltpu.roll(wide, 0, 1, stride=1, stride_axis=0).astype(bf16)
        return 0

    lax.fori_loop(0, mine, build, 0)

    for copy in halo:
        copy.wait_recv()
    for b in range(1, reach + 2):
        tile = dy_buf[b].astype(f32).reshape(block, half).astype(bf16)
        if b <= reach:
            dyc[b * block:(b + 1) * block, 0:half] = tile
        if b >= 2:
            dyc[(b - 1) * block:b * block, half:width] = tile

    lane_all = lax.rem(lax.broadcasted_iota(jnp.int32, (block, width), 1), half) // per

    def convolve(i, acc):
        filters = toep[pl.ds(i * GANG, GANG)].reshape(GANG * block, span)
        out = jnp.dot(filters, dyc[...], preferred_element_type=f32)
        for q in range(GANG):
            acc = jnp.where(lane_all == i * GANG + q, out[q * block:(q + 1) * block, :], acc)
        return acc

    grads_in = lax.fori_loop(0, mine // GANG, convolve, jnp.zeros((block, width), f32)).astype(bf16)
    for b in range(2):
        dx_out[b] = grads_in[:, b * half:(b + 1) * half]
    swap = send(dx_out.at[1 - e], dx_buf.at[e], s_dx, r_dx, sib, c)
    at = pl.ds(pl.multiple_of(e * half, half), half)
    kept = pltpu.make_async_copy(dx_out.at[e], dx_hbm.at[:, at], s_loc.at[2])
    kept.start()
    swap.wait_recv()
    at = pl.ds(pl.multiple_of((1 - e) * half, half), half)
    other = pltpu.make_async_copy(dx_buf.at[1 - e], dx_hbm.at[:, at], s_loc.at[3])
    other.start()

    all_terms.wait_recv()
    terms = jnp.sum(rs[...], axis=0)
    for t in range(8):
        dh_ref[t:t + 1, :] = terms[:, t * groups:(t + 1) * groups]

    kept.wait()
    other.wait()
    for copy in [*a2a.values(), *x_sends, *halo, all_rows, all_terms, swap]:
        copy.wait_send()


def on_device(ns, nc, dy, x, filt):
    rows = dy.shape[0]
    block, width = x.shape
    half = width // 2
    groups = filt.shape[1]
    taps = filt.shape[0] * ns
    reach = taps // block
    span = taps + block
    zs = nc // CROSS
    f32, bf16 = jnp.float32, jnp.bfloat16
    vmem, dma = pltpu.VMEM, pltpu.SemaphoreType.DMA
    return pl.pallas_call(
        functools.partial(kernel, ns, nc),
        out_shape=(jax.ShapeDtypeStruct(x.shape, bf16), jax.ShapeDtypeStruct(filt.shape, f32)),
        in_specs=[pl.BlockSpec(memory_space=pl.ANY), pl.BlockSpec(memory_space=pl.ANY),
                  pl.BlockSpec(memory_space=pltpu.VMEM)],
        out_specs=(pl.BlockSpec(memory_space=pl.ANY), pl.BlockSpec(memory_space=pltpu.VMEM)),
        scratch_shapes=[
            vmem((reach + 2, nc, rows, half), bf16),
            vmem((span, width), bf16),
            vmem((block, width), bf16),
            vmem((2, block, half), bf16),
            vmem((reach + 2, block, half), bf16),
            vmem((span, width), bf16),
            vmem((ns, 1, LANES), f32),
            vmem((ns, LANES), f32),
            vmem((taps, LANES), f32),
            vmem((groups, span), f32),
            vmem((groups // 2, block, span), bf16),
            vmem((LANES, span), f32),
            vmem((taps, LANES), f32),
            vmem((ns, LANES), f32),
            vmem((ns, 1, LANES), f32),
            vmem((ns, 1, LANES), f32),
            vmem((2, block, half), bf16),
            vmem((2, block, half), bf16),
            dma((zs, CROSS, 2)), dma((zs, CROSS, 2)),
            dma((reach // 2 + 1, 2)), dma((reach // 2 + 1, 2)),
            dma, dma,
            dma((reach // 2, zs)), dma((reach // 2, zs)),
            dma, dma, dma, dma,
            dma((4,)),
        ],
        compiler_params=pltpu.CompilerParams(
            collective_id=0, has_side_effects=True, vmem_limit_bytes=40 * 2**20),
    )(dy, x, filt)


def solution(mesh):
    ns, nc = mesh.shape["seq"], mesh.shape["chan"]
    in_specs = (P(("seq", "chan"), None), P("seq", "chan"), P("seq", "chan"))
    out_specs = (P("seq", "chan"), P("seq", "chan"))
    return jax.shard_map(
        functools.partial(on_device, ns, nc), mesh=mesh, in_specs=in_specs, out_specs=out_specs, check_vma=False)
```

time: 66.3 us -> 59 us (0.89)
  Pallas kernels: 61.8 us -> 54.6 us
    pallas_call x1, Pallas kernels: 61.8 us -> 54.6 us  [on_device(): pl.pallas_call(functools.partial(kernel, ns, nc), out_shape=(jax.ShapeDty...]
where the time goes in v2:
time: 59 us; the launch traced here: 58.8 us
  Pallas kernels  54.6 us (93%)
  local copies, waits for them, and re-layouts  3.58 us (6%)
  between operations  0.65 us (1%)
    pallas_call x1, Pallas kernels, on_device(): pl.pallas_call(functools.partial(kernel, ns, nc), out_shape=(jax.ShapeDty...  54.6 us
    unnamed x8, local copies, waits for them, and re-layouts  3.58 us

profile of v2, /device:TPU:1, one launch (start us, length us, event | category | flops | bytes accessed | tf_op | source)
XLA Modules:
  0.0 58.8 jit_solution(4294774684946545118)
XLA Ops:
  0.6 0.0 copy-start
  0.6 0.8 %copy-done = bf16[8,4096]{1,0:T(8,128)(2,1)S(1)} copy-done((bf16[8,4096]{1,0:T(8,128)(2,1)S(1)}, bf16[8,4096]{1,0:T(8,128)(2,1)}, u32[]{:S(2)}) %copy-start) | copy-done | bytes 65560
  1.5 0.0 copy-start.1
  1.5 0.8 %copy-done.1 = bf16[128,256]{1,0:T(8,128)(2,1)S(1)} copy-done((bf16[128,256]{1,0:T(8,128)(2,1)S(1)}, bf16[128,256]{1,0:T(8,128)(2,1)}, u32[]{:S(2)}) %copy-start.1) | copy-done | bytes 65560
  2.3 0.0 copy-start.2
  2.3 0.7 %copy-done.2 = bf16[8,16]{1,0:T(8,128)(2,1)S(1)} copy-done((bf16[8,16]{1,0:T(8,128)(2,1)S(1)}, bf16[8,16]{1,0:T(8,128)(2,1)}, u32[]{:S(2)}) %copy-start.2) | copy-done | bytes 280
  3.0 54.6 %shard_map.50 = (bf16[128,256]{1,0:T(8,128)(2,1)S(1)}, f32[8,16]{1,0:T(8,128)S(1)}) custom-call(bf16[8,4096]{1,0:T(8,128)(2,1)S(1)} %copy-done, bf16[128,256]{1,0:T(8,128)(2,1)S(1)} %copy-done.1, bf16[8,16]{1,0:T(8,128)(2,1)S(1)} %copy-done.2), custom_call_target="tpu_custom_call" | custom-call | tf_op jit(solution)/shard_map/pallas_call | solution.py:233
  57.6 0.6 %copy.7 = bf16[128,256]{1,0:T(8,128)(2,1)} copy(bf16[128,256]{1,0:T(8,128)(2,1)S(1)} %get-tuple-element.4) | data formatting | bytes 131072
  58.2 0.6 %copy.8 = f32[8,16]{1,0:T(8,128)} copy(f32[8,16]{1,0:T(8,128)S(1)} %get-tuple-element.5) | data formatting | bytes 1024
Async XLA Ops:
  0.6 0.8 %copy-start = (bf16[8,4096]{1,0:T(8,128)(2,1)S(1)}, bf16[8,4096]{1,0:T(8,128)(2,1)}, u32[]{:S(2)}) copy-start(bf16[8,4096]{1,0:T(8,128)(2,1)} %dy_hbm.1) | copy-start | bytes 196612
  1.5 0.8 %copy-start.1 = (bf16[128,256]{1,0:T(8,128)(2,1)S(1)}, bf16[128,256]{1,0:T(8,128)(2,1)}, u32[]{:S(2)}) copy-start(bf16[128,256]{1,0:T(8,128)(2,1)} %x_hbm.1) | copy-start | bytes 196612
  2.3 0.7 %copy-start.2 = (bf16[8,16]{1,0:T(8,128)(2,1)S(1)}, bf16[8,16]{1,0:T(8,128)(2,1)}, u32[]{:S(2)}) copy-start(bf16[8,16]{1,0:T(8,128)(2,1)} %filt_ref.1) | copy-start | bytes 772

commit v3 on v2

--- a/solution.py
+++ b/solution.py
@@ -13,8 +13,8 @@
 GANG = 4
 
 
-def kernel(ns, nc, dy_hbm, x_hbm, filt_ref, dx_hbm, dh_ref,
-           dy_buf, dyc, x_buf, x_half, x_ext, xw, row_buf, gathered, unpacked, frow, toep, dh_rows, dh_cols,
+def kernel(ns, nc, dy_hbm, x_hbm, filt_hbm, dx_hbm, dh_ref,
+           filt_ref, dy_buf, dyc, x_buf, x_half, x_ext, xw, row_buf, gathered, unpacked, frow, toep, dh_rows, dh_cols,
            staged, packed, rs, dx_out, dx_buf,
            s_a2a, r_a2a, s_x, r_x, s_row, r_row, s_halo, r_halo, s_rs, r_rs, s_dx, r_dx, s_loc):
     f32, bf16 = jnp.float32, jnp.bfloat16
@@ -47,13 +47,20 @@
         return copy
 
     far = sorted(range(zs), key=lambda d: -min(d, zs - d))
-    near = far[::-1]
+    near = sorted(range(zs), key=lambda d: min(d, zs - d))
     cores = ((0, s), (1, sib))
 
     barrier = pltpu.get_barrier_semaphore()
-    friends = [(seq, chan_peer(dz, dx)) for dz in far for dx in range(CROSS) for _, seq in cores if dz or dx]
-    for friend in friends:
-        pl.semaphore_signal(barrier, inc=1, device_id=friend, device_id_type=MESH)
+
+    def greet_all(dz):
+        for dx in range(CROSS):
+            for r, seq in cores:
+                if dz or dx:
+                    pl.semaphore_signal(barrier, inc=1, device_id=(seq, chan_peer(dz, dx)), device_id_type=MESH)
+
+    for dz in far[:-1]:
+        pl.when(zh + dz < zs)(functools.partial(greet_all, dz))
+    greet_all(0)
 
     def greet(j, _):
         pl.semaphore_signal(barrier, inc=1, device_id=(lax.rem(s + j, ns), c), device_id_type=MESH)
@@ -63,11 +70,14 @@
 
     x_in = pltpu.make_async_copy(x_hbm, x_buf, s_loc.at[1])
     x_in.start()
+    filt_in = pltpu.make_async_copy(filt_hbm, filt_ref, s_loc.at[4])
+    filt_in.start()
     own = pltpu.make_async_copy(
         dy_hbm.at[:, pl.ds(pl.multiple_of(c * width + e * half, half), half)], dy_buf.at[e, c], s_loc.at[0])
     own.start()
 
     unpacked[...] = jnp.zeros_like(unpacked)
+    filt_in.wait()
     unpacked[0:8, 0:groups] = filt_ref[...].astype(f32)
     row_buf[s] = jnp.sum(pltpu.roll(unpacked[0:8, :], 0, 1, stride=groups, stride_axis=0), axis=0, keepdims=True)
     frow[...] = jnp.zeros_like(frow)
@@ -81,18 +91,25 @@
         x_half[h] = jnp.dot(flip, x_buf[:, h * half:(h + 1) * half], preferred_element_type=f32).astype(bf16)
     x_ext[1 - e] = x_half[e]
 
-    pl.semaphore_wait(barrier, len(friends) + ns - 1)
-
-    a2a = {}
-    for dz in far:
-        for dx in range(CROSS):
-            for r, seq in cores:
-                if dz or dx or r:
-                    peer = chan_peer(dz, dx)
-                    their = e if r == 0 else 1 - e
-                    start = pl.multiple_of(peer * width + their * half, half)
-                    a2a[dz, dx, r] = send(dy_hbm.at[:, pl.ds(start, half)], dy_buf.at[e, c],
-                                          s_a2a.at[dz, dx, r], r_a2a.at[dz, dx, r], seq, peer)
+    pl.semaphore_wait(barrier, 2 * (CROSS - 1) + ns - 1 + 2 * CROSS * zh)
+
+    def chunk_copy(dz, dx, r):
+        peer = chan_peer(dz, dx)
+        their = e if r == 0 else 1 - e
+        start = pl.multiple_of(peer * width + their * half, half)
+        return copy_to(dy_hbm.at[:, pl.ds(start, half)], dy_buf.at[e, c],
+                       s_a2a.at[dz, dx, r], r_a2a.at[dz, dx, r], cores[r][1], peer)
+
+    def wanted(dz):
+        return [(dz, dx, r) for dx in range(CROSS) for r in range(2) if dz or dx or r]
+
+    def send_chunks(dz):
+        for key in wanted(dz):
+            chunk_copy(*key).start()
+
+    for dz in far[:-1]:
+        pl.when(zh + dz >= zs)(functools.partial(send_chunks, dz))
+    send_chunks(0)
     x_sends = []
     for m in range(reach // 2 + 1):
         for r, seq in cores:
@@ -101,6 +118,7 @@
                 x_sends.append(send(x_half.at[their], x_ext.at[2 * m + 1 - e],
                                     s_x.at[m, r], r_x.at[m, r], lax.rem(seq + 2 * m, ns), c))
 
+
     def send_row(j, _):
         copy_to(row_buf.at[s], row_buf.at[s], s_row, r_row, lax.rem(s + j, ns), c).start()
         return 0
@@ -114,16 +132,16 @@
     halo = []
     total = jnp.zeros((mine, span), f32)
     for dz in near:
-        for dx in range(CROSS):
-            for r, _ in cores:
-                if dz or dx or r:
-                    a2a[dz, dx, r].wait_recv()
-        zg = lax.rem(zh + zs - dz, zs)
+        for key in wanted((zs - dz) % zs):
+            chunk_copy(*key).wait_recv()
+        zg = lax.rem(zh + dz, zs)
         part = (pl.ds(0, 2), pl.ds(zg * CROSS, CROSS))
         for m in range(1, reach // 2 + 1):
             halo.append(send(dy_buf.at[part], dy_buf.at[pl.ds(2 * m, 2), pl.ds(zg * CROSS, CROSS)],
                              s_halo.at[m - 1, dz], r_halo.at[m - 1, dz], lax.rem(s + ns - 2 * m, ns), c))
-        if dz == 0:
+        if dz:
+            pl.when(zh + dz < zs)(functools.partial(send_chunks, dz))
+        else:
             for copy in x_sends:
                 copy.wait_recv()
             for i in range(reach + 1):
@@ -215,7 +233,10 @@
 
     kept.wait()
     other.wait()
-    for copy in [*a2a.values(), *x_sends, *halo, all_rows, all_terms, swap]:
+    for dz in range(zs):
+        for key in wanted(dz):
+            chunk_copy(*key).wait_send()
+    for copy in [*x_sends, *halo, all_rows, all_terms, swap]:
         copy.wait_send()
 
 
@@ -233,10 +254,10 @@
     return pl.pallas_call(
         functools.partial(kernel, ns, nc),
         out_shape=(jax.ShapeDtypeStruct(x.shape, bf16), jax.ShapeDtypeStruct(filt.shape, f32)),
-        in_specs=[pl.BlockSpec(memory_space=pl.ANY), pl.BlockSpec(memory_space=pl.ANY),
-                  pl.BlockSpec(memory_space=pltpu.VMEM)],
+        in_specs=[pl.BlockSpec(memory_space=pltpu.HBM)] * 3,
         out_specs=(pl.BlockSpec(memory_space=pl.ANY), pl.BlockSpec(memory_space=pltpu.VMEM)),
         scratch_shapes=[
+            vmem(filt.shape, bf16),
             vmem((reach + 2, nc, rows, half), bf16),
             vmem((span, width), bf16),
             vmem((block, width), bf16),
@@ -260,10 +281,10 @@
             dma, dma,
             dma((reach // 2, zs)), dma((reach // 2, zs)),
             dma, dma, dma, dma,
-            dma((4,)),
+            dma((5,)),
         ],
         compiler_params=pltpu.CompilerParams(
-            collective_id=0, has_side_effects=True, vmem_limit_bytes=40 * 2**20),
+            collective_id=0, has_side_effects=True, vmem_limit_bytes=60 * 2**20),
     )(dy, x, filt)
 
 

time: 59 us -> 57.3 us (0.971)
  the two profiles are of different devices: /device:TPU:1 before, /device:TPU:769 now
where the time goes in v3:
time: 57.3 us; the launch traced here: 57.1 us
  Pallas kernels  54.4 us (95%)
  local copies, waits for them, and re-layouts  2.07 us (4%)
  between operations  0.65 us (1%)
    pallas_call x1, Pallas kernels, on_device(): pl.pallas_call(functools.partial(kernel, ns, nc), out_shape=(jax.ShapeDty...  54.4 us
    unnamed x4, local copies, waits for them, and re-layouts  2.07 us

profile of v3, /device:TPU:769, one launch (start us, length us, event | category | flops | bytes accessed | tf_op | source)
XLA Modules:
  0.0 57.1 jit_solution(12747964530476014843)
XLA Ops:
  0.6 54.4 %shard_map.50 = (bf16[128,256]{1,0:T(8,128)(2,1)}, f32[8,16]{1,0:T(8,128)}) custom-call(bf16[8,4096]{1,0:T(8,128)(2,1)} %dy_hbm.1, bf16[128,256]{1,0:T(8,128)(2,1)} %x_hbm.1, bf16[8,16]{1,0:T(8,128)(2,1)} %filt_hbm.1), custom_call_target="tpu_custom_call" | custom-call | tf_op jit(solution)/shard_map/pallas_call | solution.py:254
  55.0 0.0 copy-start
  55.0 1.5 %copy.7 = bf16[128,256]{1,0:T(8,128)(2,1)} copy(bf16[128,256]{1,0:T(8,128)(2,1)} %get-tuple-element.4) | data formatting | bytes 131072
  56.5 0.0 copy-done
  56.5 0.6 %copy.8 = f32[8,16]{1,0:T(8,128)} copy(f32[8,16]{1,0:T(8,128)S(1)} %copy-done) | data formatting | bytes 1024
Async XLA Ops:
  55.0 1.5 %copy-start = (f32[8,16]{1,0:T(8,128)S(1)}, f32[8,16]{1,0:T(8,128)}, u32[]{:S(2)}) copy-start(f32[8,16]{1,0:T(8,128)} %get-tuple-element.5) | copy-start | bytes 1540

commit v4 on v3

--- a/solution.py
+++ b/solution.py
@@ -9,14 +9,15 @@
 
 MESH = pl.DeviceIdType.MESH
 LANES = 128
+INNER = 8
 CROSS = 4
 GANG = 4
 
 
 def kernel(ns, nc, dy_hbm, x_hbm, filt_hbm, dx_hbm, dh_ref,
            filt_ref, dy_buf, dyc, x_buf, x_half, x_ext, xw, row_buf, gathered, unpacked, frow, toep, dh_rows, dh_cols,
-           staged, packed, rs, dx_out, dx_buf,
-           s_a2a, r_a2a, s_x, r_x, s_row, r_row, s_halo, r_halo, s_rs, r_rs, s_dx, r_dx, s_loc):
+           staged, packed, rs, dx_out, dx_buf, relayed,
+           s_a2a, r_a2a, s_rel, r_rel, s_fwd, r_fwd, s_x, r_x, s_row, r_row, s_halo, r_halo, s_rs, r_rs, s_dx, r_dx, s_loc):
     f32, bf16 = jnp.float32, jnp.bfloat16
     zs = nc // CROSS
     rows, half = dy_buf.shape[2], dy_buf.shape[3]
@@ -32,6 +33,7 @@
     s, c = lax.axis_index("seq"), lax.axis_index("chan")
     e = lax.rem(s, 2)
     sib = s + 1 - 2 * e
+    outer, zo, yc = ns // INNER, s // INNER, lax.rem(s, INNER)
     zh, xx = c // CROSS, lax.rem(c, CROSS)
 
     def chan_peer(dz, dx):
@@ -63,10 +65,14 @@
     greet_all(0)
 
     def greet(j, _):
-        pl.semaphore_signal(barrier, inc=1, device_id=(lax.rem(s + j, ns), c), device_id_type=MESH)
+        pl.semaphore_signal(barrier, inc=1, device_id=(j, c), device_id_type=MESH)
         return 0
 
-    lax.fori_loop(1, ns, greet, 0)
+    def greet_inner(j, _):
+        return greet(zo * INNER + lax.rem(yc + j, INNER), 0)
+
+    lax.fori_loop(0, zo * INNER, greet, 0)
+    lax.fori_loop(1, INNER, greet_inner, 0)
 
     x_in = pltpu.make_async_copy(x_hbm, x_buf, s_loc.at[1])
     x_in.start()
@@ -76,6 +82,49 @@
         dy_hbm.at[:, pl.ds(pl.multiple_of(c * width + e * half, half), half)], dy_buf.at[e, c], s_loc.at[0])
     own.start()
 
+    pl.semaphore_wait(barrier, 2 * (CROSS - 1) + INNER - 1 + INNER * (outer - 1 - zo) + 2 * CROSS * zh)
+
+    def chunk_copy(dz, dx, r):
+        peer = chan_peer(dz, dx)
+        their = e if r == 0 else 1 - e
+        start = pl.multiple_of(peer * width + their * half, half)
+        return copy_to(dy_hbm.at[:, pl.ds(start, half)], dy_buf.at[e, c],
+                       s_a2a.at[dz, dx, r], r_a2a.at[dz, dx, r], cores[r][1], peer)
+
+    def wanted(dz):
+        return [(dz, dx, r) for dx in range(CROSS) for r in range(2) if dz or dx or r]
+
+    def send_chunks(dz):
+        for key in wanted(dz):
+            chunk_copy(*key).start()
+
+    via = lax.rem(zs + 1 - zh, zs)
+
+    def relay_copy(dx, r):
+        column = lax.rem(xx + dx, CROSS)
+        their = e if r == 0 else 1 - e
+        start = pl.multiple_of(((zh + 2) * CROSS + column) * width + their * half, half)
+        return copy_to(dy_hbm.at[:, pl.ds(start, half)], relayed.at[e, xx],
+                       s_rel.at[dx, r], r_rel.at[dx, r], cores[r][1], via * CROSS + column)
+
+    relays = [(dx, r) for dx in range(CROSS) for r in range(2)]
+
+    def send_relays():
+        for key in relays:
+            relay_copy(*key).start()
+
+    forward = copy_to(relayed, dy_buf.at[pl.ds(0, 2), pl.ds(via * CROSS, CROSS)], s_fwd, r_fwd,
+                      s, (3 - zh) * CROSS + xx)
+
+    def send_forward():
+        for key in relays:
+            relay_copy(*key).wait_recv()
+        forward.start()
+
+    for dz in range(1, zs):
+        pl.when(zh + dz == zs)(functools.partial(send_chunks, dz))
+    send_chunks(0)
+
     unpacked[...] = jnp.zeros_like(unpacked)
     filt_in.wait()
     unpacked[0:8, 0:groups] = filt_ref[...].astype(f32)
@@ -91,57 +140,98 @@
         x_half[h] = jnp.dot(flip, x_buf[:, h * half:(h + 1) * half], preferred_element_type=f32).astype(bf16)
     x_ext[1 - e] = x_half[e]
 
-    pl.semaphore_wait(barrier, 2 * (CROSS - 1) + ns - 1 + 2 * CROSS * zh)
-
-    def chunk_copy(dz, dx, r):
-        peer = chan_peer(dz, dx)
+    def x_copy(m, r):
         their = e if r == 0 else 1 - e
-        start = pl.multiple_of(peer * width + their * half, half)
-        return copy_to(dy_hbm.at[:, pl.ds(start, half)], dy_buf.at[e, c],
-                       s_a2a.at[dz, dx, r], r_a2a.at[dz, dx, r], cores[r][1], peer)
-
-    def wanted(dz):
-        return [(dz, dx, r) for dx in range(CROSS) for r in range(2) if dz or dx or r]
-
-    def send_chunks(dz):
-        for key in wanted(dz):
-            chunk_copy(*key).start()
-
-    for dz in far[:-1]:
-        pl.when(zh + dz >= zs)(functools.partial(send_chunks, dz))
-    send_chunks(0)
-    x_sends = []
-    for m in range(reach // 2 + 1):
-        for r, seq in cores:
-            if m or r:
-                their = e if r == 0 else 1 - e
-                x_sends.append(send(x_half.at[their], x_ext.at[2 * m + 1 - e],
-                                    s_x.at[m, r], r_x.at[m, r], lax.rem(seq + 2 * m, ns), c))
-
+        return copy_to(x_half.at[their], x_ext.at[2 * m + 1 - e], s_x.at[m, r], r_x.at[m, r],
+                       lax.rem(cores[r][1] + 2 * m, ns), c)
+
+    def send_x(m):
+        for r in range(2):
+            x_copy(m, r).start()
+
+    x_copy(0, 1).start()
+    later = range(1, reach // 2 + 1)
+    for m in later:
+        pl.when(s // 2 + m < ns // 2)(functools.partial(send_x, m))
+    x_sends = [x_copy(0, 1)] + [x_copy(m, r) for m in later for r in range(2)]
 
     def send_row(j, _):
-        copy_to(row_buf.at[s], row_buf.at[s], s_row, r_row, lax.rem(s + j, ns), c).start()
+        copy_to(row_buf.at[s], row_buf.at[s], s_row, r_row.at[zo], j, c).start()
         return 0
 
-    lax.fori_loop(1, ns, send_row, 0)
-    all_rows = copy_to(row_buf.at[pl.ds(0, ns - 1)], row_buf.at[pl.ds(0, ns - 1)], s_row, r_row, sib, c)
+    def send_row_inner(j, _):
+        return send_row(zo * INNER + lax.rem(yc + j, INNER), 0)
+
+    def rows_of(k, count):
+        return copy_to(row_buf.at[pl.ds(0, count)], row_buf.at[pl.ds(0, count)], s_row, r_row.at[k], sib, c)
+
+    lax.fori_loop(1, INNER, send_row_inner, 0)
+    lax.fori_loop((zo + 1) * INNER, ns, send_row, 0)
+    pl.when(zh == 1)(send_relays)
+    for dz in range(1, zs):
+        pl.when(zh + dz > zs)(functools.partial(send_chunks, dz))
 
     lane = lax.broadcasted_iota(jnp.int32, (quarter, width), 1)
     lane_group = lax.rem(lane, half) // per
+
+    def answer(k, _):
+        rows_of(k, INNER).wait_recv()
+        return lax.fori_loop(k * INNER, (k + 1) * INNER, send_row, 0)
+
+    lax.fori_loop(0, zo, answer, 0)
+    for m in later:
+        pl.when(s // 2 + m >= ns // 2)(functools.partial(send_x, m))
+
+    def toeplitz():
+        rows_of(zo, INNER - 1).wait_recv()
+
+        def rest(k, _):
+            rows_of(k, INNER).wait_recv()
+            return 0
+
+        lax.fori_loop(zo + 1, outer, rest, 0)
+        for i in range(ns):
+            gathered[i:i + 1, :] = row_buf[i]
+        for t in range(8):
+            turned = gathered[...] if t == 0 else pltpu.roll(gathered[...], LANES - t * groups, 1)
+            unpacked[pl.ds(t, ns, stride=8), :] = turned
+        for b in range(taps // LANES):
+            frow[:, b * LANES:(b + 1) * LANES] = unpacked[b * LANES:(b + 1) * LANES, :].T[0:groups, :]
+
+        def build(g, _):
+            wide = jnp.broadcast_to(frow[pl.ds(e * mine + g, 1), :], (block, span))
+            toep[g] = pltpu.roll(wide, 0, 1, stride=1, stride_axis=0).astype(bf16)
+            return 0
+
+        lax.fori_loop(0, mine, build, 0)
+
     own.wait()
     halo = []
     total = jnp.zeros((mine, span), f32)
     for dz in near:
-        for key in wanted((zs - dz) % zs):
-            chunk_copy(*key).wait_recv()
+        if dz == near[-1]:
+            toeplitz()
+        def await_chunks(dz=dz):
+            for key in wanted((zs - dz) % zs):
+                chunk_copy(*key).wait_recv()
+
+        if dz == 2:
+            pl.when(zh < 2)(await_chunks)
+            pl.when(zh >= 2)(forward.wait_recv)
+        else:
+            await_chunks()
         zg = lax.rem(zh + dz, zs)
         part = (pl.ds(0, 2), pl.ds(zg * CROSS, CROSS))
         for m in range(1, reach // 2 + 1):
             halo.append(send(dy_buf.at[part], dy_buf.at[pl.ds(2 * m, 2), pl.ds(zg * CROSS, CROSS)],
                              s_halo.at[m - 1, dz], r_halo.at[m - 1, dz], lax.rem(s + ns - 2 * m, ns), c))
-        if dz:
+        if dz == 1:
             pl.when(zh + dz < zs)(functools.partial(send_chunks, dz))
-        else:
+            pl.when(zh == 0)(send_relays)
+        elif dz == 3:
+            pl.when(zh + dz < zs)(functools.partial(send_chunks, dz))
+            pl.when(zh < 2)(send_forward)
+        elif dz == 0:
             for copy in x_sends:
                 copy.wait_recv()
             for i in range(reach + 1):
@@ -180,22 +270,6 @@
     rs[0] = packed[s]
     all_terms = copy_to(packed.at[pl.ds(0, ns - 1)], rs.at[pl.ds(1, ns - 1)], s_rs, r_rs, sib, c)
 
-    all_rows.wait_recv()
-    for i in range(ns):
-        gathered[i:i + 1, :] = row_buf[i]
-    for t in range(8):
-        turned = gathered[...] if t == 0 else pltpu.roll(gathered[...], LANES - t * groups, 1)
-        unpacked[pl.ds(t, ns, stride=8), :] = turned
-    for b in range(taps // LANES):
-        frow[:, b * LANES:(b + 1) * LANES] = unpacked[b * LANES:(b + 1) * LANES, :].T[0:groups, :]
-
-    def build(g, _):
-        wide = jnp.broadcast_to(frow[pl.ds(e * mine + g, 1), :], (block, span))
-        toep[g] = pltpu.roll(wide, 0, 1, stride=1, stride_axis=0).astype(bf16)
-        return 0
-
-    lax.fori_loop(0, mine, build, 0)
-
     for copy in halo:
         copy.wait_recv()
     for b in range(1, reach + 2):
@@ -233,10 +307,23 @@
 
     kept.wait()
     other.wait()
-    for dz in range(zs):
+    def await_sends(dz):
         for key in wanted(dz):
             chunk_copy(*key).wait_send()
-    for copy in [*x_sends, *halo, all_rows, all_terms, swap]:
+
+    for dz in range(zs):
+        if dz != 2:
+            await_sends(dz)
+    pl.when(zh >= 2)(functools.partial(await_sends, 2))
+
+    def await_relays():
+        for key in relays:
+            relay_copy(*key).wait_send()
+        forward.wait_send()
+
+    pl.when(zh < 2)(await_relays)
+    rows_of(zo, ns - 1).wait_send()
+    for copy in [*x_sends, *halo, all_terms, swap]:
         copy.wait_send()
 
 
@@ -276,9 +363,11 @@
             vmem((ns, 1, LANES), f32),
             vmem((2, block, half), bf16),
             vmem((2, block, half), bf16),
+            vmem((2, CROSS, rows, half), bf16),
             dma((zs, CROSS, 2)), dma((zs, CROSS, 2)),
+            dma((CROSS, 2)), dma((CROSS, 2)), dma, dma,
             dma((reach // 2 + 1, 2)), dma((reach // 2 + 1, 2)),
-            dma, dma,
+            dma, dma((ns // INNER,)),
             dma((reach // 2, zs)), dma((reach // 2, zs)),
             dma, dma, dma, dma,
             dma((5,)),

time: 57.3 us -> 55.4 us (0.967)
  the two profiles are of different devices: /device:TPU:769 before, /device:TPU:1 now
where the time goes in v4:
time: 55.4 us; the launch traced here: 55.2 us
  Pallas kernels  52.5 us (95%)
  local copies, waits for them, and re-layouts  2.07 us (4%)
  between operations  0.65 us (1%)
    pallas_call x1, Pallas kernels, on_device(): pl.pallas_call(functools.partial(kernel, ns, nc), out_shape=(jax.ShapeDty...  52.5 us
    unnamed x4, local copies, waits for them, and re-layouts  2.07 us

profile of v4, /device:TPU:1, one launch (start us, length us, event | category | flops | bytes accessed | tf_op | source)
XLA Modules:
  0.0 55.2 jit_solution(95083570335232096)
XLA Ops:
  0.6 52.5 %shard_map.50 = (bf16[128,256]{1,0:T(8,128)(2,1)}, f32[8,16]{1,0:T(8,128)}) custom-call(bf16[8,4096]{1,0:T(8,128)(2,1)} %dy_hbm.1, bf16[128,256]{1,0:T(8,128)(2,1)} %x_hbm.1, bf16[8,16]{1,0:T(8,128)(2,1)} %filt_hbm.1), custom_call_target="tpu_custom_call" | custom-call | tf_op jit(solution)/shard_map/pallas_call | solution.py:341
  53.1 0.0 copy-start
  53.1 1.5 %copy.7 = bf16[128,256]{1,0:T(8,128)(2,1)} copy(bf16[128,256]{1,0:T(8,128)(2,1)} %get-tuple-element.4) | data formatting | bytes 131072
  54.6 0.0 copy-done
  54.6 0.6 %copy.8 = f32[8,16]{1,0:T(8,128)} copy(f32[8,16]{1,0:T(8,128)S(1)} %copy-done) | data formatting | bytes 1024
Async XLA Ops:
  53.1 1.5 %copy-start = (f32[8,16]{1,0:T(8,128)S(1)}, f32[8,16]{1,0:T(8,128)}, u32[]{:S(2)}) copy-start(f32[8,16]{1,0:T(8,128)} %get-tuple-element.5) | copy-start | bytes 1540

commit v5 on v4

--- a/solution.py
+++ b/solution.py
@@ -16,7 +16,7 @@
 
 def kernel(ns, nc, dy_hbm, x_hbm, filt_hbm, dx_hbm, dh_ref,
            filt_ref, dy_buf, dyc, x_buf, x_half, x_ext, xw, row_buf, gathered, unpacked, frow, toep, dh_rows, dh_cols,
-           staged, packed, rs, dx_out, dx_buf, relayed,
+           staged, packed, rs, dx_out, relayed,
            s_a2a, r_a2a, s_rel, r_rel, s_fwd, r_fwd, s_x, r_x, s_row, r_row, s_halo, r_halo, s_rs, r_rs, s_dx, r_dx, s_loc):
     f32, bf16 = jnp.float32, jnp.bfloat16
     zs = nc // CROSS
@@ -76,7 +76,7 @@
 
     x_in = pltpu.make_async_copy(x_hbm, x_buf, s_loc.at[1])
     x_in.start()
-    filt_in = pltpu.make_async_copy(filt_hbm, filt_ref, s_loc.at[4])
+    filt_in = pltpu.make_async_copy(filt_hbm, filt_ref, s_loc.at[3])
     filt_in.start()
     own = pltpu.make_async_copy(
         dy_hbm.at[:, pl.ds(pl.multiple_of(c * width + e * half, half), half)], dy_buf.at[e, c], s_loc.at[0])
@@ -291,14 +291,10 @@
     grads_in = lax.fori_loop(0, mine // GANG, convolve, jnp.zeros((block, width), f32)).astype(bf16)
     for b in range(2):
         dx_out[b] = grads_in[:, b * half:(b + 1) * half]
-    swap = send(dx_out.at[1 - e], dx_buf.at[e], s_dx, r_dx, sib, c)
     at = pl.ds(pl.multiple_of(e * half, half), half)
+    swap = send(dx_out.at[1 - e], dx_hbm.at[:, at], s_dx, r_dx, sib, c)
     kept = pltpu.make_async_copy(dx_out.at[e], dx_hbm.at[:, at], s_loc.at[2])
     kept.start()
-    swap.wait_recv()
-    at = pl.ds(pl.multiple_of((1 - e) * half, half), half)
-    other = pltpu.make_async_copy(dx_buf.at[1 - e], dx_hbm.at[:, at], s_loc.at[3])
-    other.start()
 
     all_terms.wait_recv()
     terms = jnp.sum(rs[...], axis=0)
@@ -306,7 +302,7 @@
         dh_ref[t:t + 1, :] = terms[:, t * groups:(t + 1) * groups]
 
     kept.wait()
-    other.wait()
+    swap.wait_recv()
     def await_sends(dz):
         for key in wanted(dz):
             chunk_copy(*key).wait_send()
@@ -362,7 +358,6 @@
             vmem((ns, 1, LANES), f32),
             vmem((ns, 1, LANES), f32),
             vmem((2, block, half), bf16),
-            vmem((2, block, half), bf16),
             vmem((2, CROSS, rows, half), bf16),
             dma((zs, CROSS, 2)), dma((zs, CROSS, 2)),
             dma((CROSS, 2)), dma((CROSS, 2)), dma, dma,
@@ -370,11 +365,11 @@
             dma, dma((ns // INNER,)),
             dma((reach // 2, zs)), dma((reach // 2, zs)),
             dma, dma, dma, dma,
-            dma((5,)),
+            dma((4,)),
         ],
         compiler_params=pltpu.CompilerParams(
-            collective_id=0, has_side_effects=True, vmem_limit_bytes=60 * 2**20),
-    )(dy, x, filt)
+            collective_id=0, has_side_effects=True, vmem_limit_bytes=40 * 2**20),
+    )(*(pltpu.with_memory_space_constraint(a, pltpu.HBM) for a in (dy, x, filt)))
 
 
 def solution(mesh):

time: 55.4 us -> 53.9 us (0.973)
  local copies, waits for them, and re-layouts: 2.07 us -> 1.22 us
  Pallas kernels: 52.5 us -> 51.9 us
    unnamed x4 -> x2, local copies, waits for them, and re-layouts: 2.07 us -> 1.22 us
    pallas_call x1, Pallas kernels: 52.5 us -> 51.9 us  [on_device(): pl.pallas_call(functools.partial(kernel, ns, nc), out_shape=(jax.ShapeDty...]
where the time goes in v5:
time: 53.9 us; the launch traced here: 53.7 us
  Pallas kernels  51.9 us (96%)
  local copies, waits for them, and re-layouts  1.22 us (2%)
  between operations  0.64 us (1%)
    pallas_call x1, Pallas kernels, on_device(): pl.pallas_call(functools.partial(kernel, ns, nc), out_shape=(jax.ShapeDty...  51.9 us
    unnamed x2, local copies, waits for them, and re-layouts  1.22 us

profile of v5, /device:TPU:1, one launch (start us, length us, event | category | flops | bytes accessed | tf_op | source)
XLA Modules:
  0.0 53.7 jit_solution(18155381761692721395)
XLA Ops:
  0.6 51.9 %shard_map.50 = (bf16[128,256]{1,0:T(8,128)(2,1)S(1)}, f32[8,16]{1,0:T(8,128)S(1)}) custom-call(bf16[8,4096]{1,0:T(8,128)(2,1)} %dy_hbm.1, bf16[128,256]{1,0:T(8,128)(2,1)} %x_hbm.1, bf16[8,16]{1,0:T(8,128)(2,1)} %filt_hbm.1), custom_call_target="tpu_custom_call" | custom-call | tf_op jit(solution)/shard_map/pallas_call | solution.py:337
  52.5 0.6 %copy.7 = bf16[128,256]{1,0:T(8,128)(2,1)} copy(bf16[128,256]{1,0:T(8,128)(2,1)S(1)} %get-tuple-element.4) | data formatting | bytes 131072
  53.1 0.6 %copy.8 = f32[8,16]{1,0:T(8,128)} copy(f32[8,16]{1,0:T(8,128)S(1)} %get-tuple-element.5) | data formatting | bytes 1024

commit v6 on v5

--- a/solution.py
+++ b/solution.py
@@ -261,12 +261,14 @@
     for i in range(ns):
         packed[i] = staged[i:i + 1, :]
 
-    def send_terms(j, _):
-        peer = lax.rem(s + j, ns)
-        copy_to(packed.at[peer], rs.at[j], s_rs, r_rs, peer, c).start()
+    def send_terms(i, _):
+        for u in range(INNER - 1):
+            j = 1 + i * (INNER - 1) + u
+            peer = lax.rem(s + j, ns)
+            copy_to(packed.at[peer], rs.at[j], s_rs, r_rs, peer, c).start()
         return 0
 
-    lax.fori_loop(1, ns, send_terms, 0)
+    lax.fori_loop(0, (ns - 1) // (INNER - 1), send_terms, 0)
     rs[0] = packed[s]
     all_terms = copy_to(packed.at[pl.ds(0, ns - 1)], rs.at[pl.ds(1, ns - 1)], s_rs, r_rs, sib, c)
 

time: 53.9 us -> 53.8 us (level)
  no operation moved by 1% of the time
where the time goes in v6:
time: 53.8 us; the launch traced here: 53.7 us
  Pallas kernels  51.8 us (96%)
  local copies, waits for them, and re-layouts  1.22 us (2%)
  between operations  0.64 us (1%)
    pallas_call x1, Pallas kernels, on_device(): pl.pallas_call(functools.partial(kernel, ns, nc), out_shape=(jax.ShapeDty...  51.8 us
    unnamed x2, local copies, waits for them, and re-layouts  1.22 us

profile of v6, /device:TPU:1, one launch (start us, length us, event | category | flops | bytes accessed | tf_op | source)
XLA Modules:
  0.0 53.7 jit_solution(2867205222244999498)
XLA Ops:
  0.6 51.8 %shard_map.50 = (bf16[128,256]{1,0:T(8,128)(2,1)S(1)}, f32[8,16]{1,0:T(8,128)S(1)}) custom-call(bf16[8,4096]{1,0:T(8,128)(2,1)} %dy_hbm.1, bf16[128,256]{1,0:T(8,128)(2,1)} %x_hbm.1, bf16[8,16]{1,0:T(8,128)(2,1)} %filt_hbm.1), custom_call_target="tpu_custom_call" | custom-call | tf_op jit(solution)/shard_map/pallas_call | solution.py:339
  52.5 0.6 %copy.7 = bf16[128,256]{1,0:T(8,128)(2,1)} copy(bf16[128,256]{1,0:T(8,128)(2,1)S(1)} %get-tuple-element.4) | data formatting | bytes 131072
  53.1 0.6 %copy.8 = f32[8,16]{1,0:T(8,128)} copy(f32[8,16]{1,0:T(8,128)S(1)} %get-tuple-element.5) | data formatting | bytes 1024
